TPU v7x, 128 devices: a whole 4x4x4 slice. The times are simulated.
128 devices in a mesh: tm: 32 (over x, y, z_hi), tensor: 4 (over z_lo, core).
Axes of the slice: x: 4, y: 4, z: 4 (z_hi: 2, z_lo: 2; z = z_hi * 2 + z_lo), core: 2. Of those that a mesh axis runs over, the one named last changes fastest.
Arguments:
- frames: bfloat16 [16384, 1408], P('tm'), may hold values from -6 to 6
- gain_attn: float32 [1408], replicated, may hold values from 0.25 to 1.75
- w_qkv: bfloat16 [1408, 3, 1408], P('tm', None, 'tensor')
- w_out: bfloat16 [1408, 1408], P('tensor', 'tm'), may hold values from -0.625 to 0.625
- gain_mlp: float32 [1408], replicated, may hold values from 0.25 to 1.75
- w_up: bfloat16 [1408, 6144], P('tm', 'tensor'), may hold values from -0.15625 to 0.15625
- w_down: bfloat16 [6144, 1408], P('tensor', 'tm'), may hold values from -0.078125 to 0.078125
- w_proj: bfloat16 [1408, 4096], P('tm', 'tensor'), may hold values from -0.15625 to 0.15625
- windows: int32 [256, 8], P('tm'), may hold values from 0 to 255, as said below
- pool_map: int32 [16384], P('tm'), may hold values from 0 to 15, as said below
- owners: int32 [4096, 1], P('tm'), may hold values from 0 to 31; in each aligned block of 128 rows (0 to 127, 128 to 255, ...) at most 8 rows name the same one
Outputs:
- received: bfloat16 [32, 256, 4096], P('tm', None, 'tensor')
Inputs may be any that keep to these rules, and one draw needn't show every extreme that they name: `windows`: row b lists 8 different blocks, each in the frame of block b or in the frame just before or just after it; frame f holds blocks 256 / 64 f onward. `pool_map`: in each aligned block of 64 patches every slot value is named by exactly 4 patches. `owners`: among the 128 rows of one index of tm no owner is named more than 8 times.
All inputs are finite; a program needn't handle non-finite values.
Results may differ from a plain program's by a relative error of at most 0.014.
The roundings to bfloat16 on the way count: a program that leaves them out, or rounds other values in their place, can miss the bound.
Values may be sent and summed in bfloat16 or wider, within the bound.
A program may use at most 64 MiB of HBM per device.

v0:
```python
import math
import jax
import jax.numpy as jnp
from jax import lax
from jax.sharding import PartitionSpec as P

D = 1408
HEADS = 16
PATCHES = 256
BLK = 64
WIN = 8
POOL = 4
eps = 1e-06


def with_halo(block, sides, width):
    for axis, dim in sides:
        count = lax.axis_size(axis)
        forward = [(i, i + 1) for i in range(count - 1)]
        backward = [(target, source) for source, target in forward]
        low = lax.ppermute(
            lax.slice_in_dim(block, block.shape[dim] - width, None, axis=dim), axis, forward
        )
        high = lax.ppermute(lax.slice_in_dim(block, 0, width, axis=dim), axis, backward)
        block = jnp.concatenate([low, block, high], axis=dim)
    return block


def layer_norm(values, scales):
    average = jnp.mean(values, axis=-1, keepdims=True)
    centred = values - average
    spread = jnp.mean(centred * centred, axis=-1, keepdims=True)
    return (centred * lax.rsqrt(spread + eps) * scales).astype(jnp.bfloat16)


def pool_rows(values, slot_map):
    block_count = values.shape[0] // BLK
    slot_ids = jnp.arange(BLK // POOL, dtype=jnp.int32)
    chooser = (slot_map.reshape(block_count, 1, BLK) == slot_ids[None, :, None]).astype(jnp.float32)
    summed = jnp.einsum(
        "bsp,bpd->bsd",
        chooser,
        values.reshape(block_count, BLK, values.shape[1]),
        precision=lax.Precision.HIGHEST,
    )
    return (
        (summed * (1.0 / POOL))
        .reshape(block_count * (BLK // POOL), values.shape[1])
        .astype(jnp.bfloat16)
    )


def tensor_total(term):
    return lax.psum(term.astype(jnp.bfloat16), "tensor").astype(jnp.float32)


def body(
    frames, gain_attn, w_qkv, w_out, gain_mlp, w_up, w_down, w_proj, windows, pool_map, owners
):
    row_count = frames.shape[0]
    query_blocks = row_count // BLK
    head_dim = D // HEADS
    full_qkv, full_out, full_up, full_down, full_proj = (
        lax.all_gather(w_qkv, "tm", axis=0, tiled=True),
        lax.all_gather(w_out, "tm", axis=1, tiled=True),
        lax.all_gather(w_up, "tm", axis=0, tiled=True),
        lax.all_gather(w_down, "tm", axis=1, tiled=True),
        lax.all_gather(w_proj, "tm", axis=0, tiled=True),
    )
    local_width = full_qkv.shape[2]
    heads_here = local_width // head_dim
    normed = layer_norm(frames.astype(jnp.float32), gain_attn)
    projected_qkv = jnp.dot(
        normed, full_qkv.reshape(D, 3 * local_width), preferred_element_type=jnp.float32
    ).astype(jnp.bfloat16)
    projected_qkv = projected_qkv.reshape(row_count, 3, local_width)
    keyvals = with_halo(projected_qkv[:, 1:, :], (("tm", 0),), PATCHES)
    per_frame = PATCHES // BLK
    kv_blocks = keyvals.reshape(query_blocks + 2 * per_frame, BLK, 2, heads_here, head_dim)
    local_ids = windows - (lax.axis_index("tm") * query_blocks - per_frame)
    group_size = math.gcd(query_blocks, 8)
    queries = projected_qkv[:, 0, :].reshape(
        query_blocks // group_size, group_size, BLK, heads_here, head_dim
    )
    score_scale = head_dim ** (-0.5)

    def attend_group(packed):
        query_group, id_group = packed
        picked = kv_blocks[id_group].reshape(group_size, WIN * BLK, 2, heads_here, head_dim)
        scores = (
            jnp.einsum(
                "gqhd,gkhd->ghqk", query_group, picked[:, :, 0], preferred_element_type=jnp.float32
            )
            * score_scale
        )
        row_top = jnp.max(scores, axis=-1, keepdims=True)
        expw = jnp.exp(scores - row_top)
        attn_probs = (expw / jnp.sum(expw, axis=-1, keepdims=True)).astype(jnp.bfloat16)
        return jnp.einsum(
            "ghqk,gkhd->gqhd", attn_probs, picked[:, :, 1], preferred_element_type=jnp.float32
        ).astype(jnp.bfloat16)

    attended = lax.map(
        attend_group, (queries, local_ids.reshape(query_blocks // group_size, group_size, WIN))
    ).reshape(row_count, local_width)
    mixed_term = jnp.dot(attended, full_out, preferred_element_type=jnp.float32)
    stream = frames.astype(jnp.float32) + tensor_total(mixed_term)
    hidden = layer_norm(stream, gain_mlp)
    activation = jax.nn.gelu(
        jnp.dot(hidden, full_up, preferred_element_type=jnp.float32), approximate=False
    ).astype(jnp.bfloat16)
    stream = stream + tensor_total(
        jnp.dot(activation, full_down, preferred_element_type=jnp.float32)
    )
    pooled = pool_rows(stream, pool_map)
    proj_rows = jnp.dot(pooled, full_proj, preferred_element_type=jnp.float32).astype(jnp.bfloat16)
    pooled_count = proj_rows.shape[0]
    owner_count = lax.axis_size("tm")
    capacity = 2 * pooled_count // owner_count
    owner_ids = owners[:, 0]
    owner_hits = (owner_ids[:, None] == jnp.arange(owner_count, dtype=jnp.int32)[None, :]).astype(
        jnp.int32
    )
    slot_rank = jnp.sum((jnp.cumsum(owner_hits, axis=0) - 1) * owner_hits, axis=1)
    slot_dest = owner_ids * capacity + slot_rank
    placement = (
        jnp.arange(owner_count * capacity, dtype=jnp.int32)[:, None] == slot_dest[None, :]
    ).astype(jnp.bfloat16)
    outbox = jnp.dot(placement, proj_rows, preferred_element_type=jnp.float32).astype(jnp.bfloat16)
    outbox = outbox.reshape(owner_count, capacity, proj_rows.shape[1])
    received = lax.all_to_all(outbox, "tm", split_axis=0, concat_axis=0, tiled=True)
    return received.reshape(1, owner_count * capacity, proj_rows.shape[1])


def solution(mesh):
    placed = (
        P("tm", None),
        P(),
        P("tm", None, "tensor"),
        P("tensor", "tm"),
        P(),
        P("tm", "tensor"),
        P("tensor", "tm"),
        P("tm", "tensor"),
        P("tm", None),
        P("tm"),
        P("tm", None),
    )
    return jax.shard_map(
        body, mesh=mesh, in_specs=placed, out_specs=P("tm", None, "tensor"), check_vma=False
    )
```

profile of v0, /device:TPU:0, one launch (start us, length us, event | category | flops | bytes accessed | tf_op | source)
XLA Modules:
  0.0 647.8 jit_solution(6431842312539559043)
XLA Ops:
  6.5 1.6 copy.23
  9.0 1.6 convert_reduce_fusion
  10.6 1.9 fusion.16
  12.5 83.1 %all-gather.9.cloned.1.call-done = bf16[1408,3,352]{2,1,0:T(4,128)(2,1)} async-done(((bf16[44,3,352]{2,1,0:T(4,128)(2,1)}), bf16[1408,3,352]{2,1,0:T(4,128)(2,1)}) %all-gather.9.cloned.1.call-update) | async-done | bytes 2973712 | tf_op jit(solution)/shard_map/all_gather | solution.py:64
  95.6 7.7 %copy.24 = bf16[1408,3,352]{0,2,1:T(8,128)(2,1)} copy(bf16[1408,3,352]{2,1,0:T(4,128)(2,1)} %all-gather.9.cloned.1.call-done) | data formatting | bytes 5947392 | tf_op jit(solution)/shard_map/all_gather | solution.py:64
  103.3 3.9 convolution_convert_fusion.2
  108.4 2.3 collective-permute-start
  113.0 102.0 %all-gather = bf16[32,44,352]{2,1,0:T(8,128)(2,1)S(1)} all-gather(bf16[1,44,352]{2,1,0:T(8,128)(2,1)S(1)} %bitcast.53), channel_id=1, replica_groups=mesh['tm'=32,'tensor'=4] {'tm'}, dimensions={0}, use_global_device_ids=true | all-gather | bytes 1022208 | tf_op jit(solution)/shard_map/all_gather | solution.py:65
  222.2 2.3 reshape.72
  224.5 2.1 copy.28
  226.6 5.5 gather_fusion
  232.2 9.4 %copy.29 = bf16[64,64,2,4,88]{4,1,0,3,2:T(8,128)(2,1)} copy(bf16[64,64,2,4,88]{4,1,3,2,0:T(8,128)(2,1)} %gather_fusion) | data formatting | bytes 11534336 | tf_op jit(solution)/shard_map/while/body/eval_jaxpr/gather | solution.py:89
  241.5 5.9 fusion.110
  247.4 6.2 copy.40
  253.6 2.6 fusion.19
  256.2 2.8 fusion.112
  259.0 6.1 copy.38
  265.1 4.4 fusion.72
  270.3 2.0 convolution_convert_fusion.1
  274.6 41.4 %all-reduce.3.cloned.1.call-done = bf16[512,1408]{1,0:T(8,128)(2,1)} async-done(((bf16[512,1408]{1,0:T(8,128)(2,1)}), bf16[512,1408]{1,0:T(8,128)(2,1)}) %all-reduce.3.cloned.1.call-update) | async-done | bytes 1441808 | tf_op jit(solution)/shard_map/psum | solution.py:54
  315.9 1.9 fusion.24
  318.5 86.1 %all-gather.11.cloned.1.call-done = bf16[32,44,1536]{2,1,0:T(8,128)(2,1)} async-done(((bf16[1,44,1536]{2,1,0:T(8,128)(2,1)}), bf16[32,44,1536]{2,1,0:T(8,128)(2,1)}) %all-gather.11.cloned.1.call-update) | async-done | bytes 4325392 | tf_op jit(solution)/shard_map/all_gather | solution.py:66
  404.6 7.0 %reshape.92 = bf16[1408,1536]{1,0:T(8,128)(2,1)} reshape(bf16[32,44,1536]{2,1,0:T(8,128)(2,1)} %all-gather.11.cloned.1.call-done) | data formatting | bytes 8650752
  411.7 77.3 %all-gather.13.cloned.1.call-done = bf16[32,44,1536]{2,1,0:T(8,128)(2,1)} async-done(((bf16[1,44,1536]{2,1,0:T(8,128)(2,1)}), bf16[32,44,1536]{2,1,0:T(8,128)(2,1)}) %all-gather.13.cloned.1.call-update) | async-done | bytes 4325392 | tf_op jit(solution)/shard_map/all_gather | solution.py:67
  488.9 7.0 %reshape.94 = bf16[1408,1536]{1,0:T(8,128)(2,1)} reshape(bf16[32,44,1536]{2,1,0:T(8,128)(2,1)} %all-gather.13.cloned.1.call-done) | data formatting | bytes 8650752
  496.0 15.1 %convolution_convert_fusion = bf16[512,1408]{1,0:T(8,128)(2,1)} fusion(bf16[1408,1536]{1,0:T(8,128)(2,1)} %reshape.94, bf16[1408,1536]{1,0:T(8,128)(2,1)} %reshape.92, bf16[512,1408]{1,0:T(8,128)(2,1)S(1)} %copy-done.1, bf16[512,1408]{1,0:T(8,128)(2,1)S(1)} %copy-done, f32[1408]{0:T(1024)S(1)} %copy-done.9, f32[512]{0:T(512)S(1)} %add_rsqrt_fusion, ...), kind=kOutput, calls=%fused_computation.30 | convolution fusion | flops 4486070272 | bytes 12985856 | tf_op jit(solution)/shard_map/dot_general | solution.py:113
  511.6 54.0 %all-gather.15.cloned.1.call-done = bf16[32,44,1024]{2,1,0:T(8,128)(2,1)} async-done(((bf16[1,44,1024]{2,1,0:T(8,128)(2,1)}), bf16[32,44,1024]{2,1,0:T(8,128)(2,1)}) %all-gather.15.cloned.1.call-update) | async-done | bytes 2883600 | tf_op jit(solution)/shard_map/all_gather | solution.py:68
  565.6 5.2 reshape.96
  570.8 40.6 %all-reduce.5.cloned.1.call-done = bf16[512,1408]{1,0:T(8,128)(2,1)} async-done(((bf16[512,1408]{1,0:T(8,128)(2,1)}), bf16[512,1408]{1,0:T(8,128)(2,1)}) %all-reduce.5.cloned.1.call-update) | async-done | bytes 1441808 | tf_op jit(solution)/shard_map/psum | solution.py:54
  611.5 1.8 convert_add_fusion.1
  614.4 2.6 fusion.71
  617.0 23.1 %all_to_all.5 = bf16[32,8,1024]{2,1,0:T(8,128)(2,1)S(1)} all-to-all(bf16[32,8,1024]{2,1,0:T(8,128)(2,1)S(1)} %fusion.71), channel_id=1, replica_groups=mesh['tm'=32,'tensor'=4] {'tm'}, dimensions={0} | all-to-all | bytes 1048576 | tf_op jit(solution)/shard_map/all_to_all | solution.py:131
  (61 shorter events, 17.5 us)
Async XLA Ops:
  6.5 89.1 %all-gather.9.cloned.1.call-start = ((), (), s32[]{:S(2)}) async-start(), calls=%async_computation.1 | async-start | bytes 4460544 | tf_op jit(solution)/shard_map/all_gather | solution.py:64
  8.2 307.8 %all-reduce.3.cloned.1.call-start = ((), (), s32[]{:S(2)}) async-start(), calls=%async_computation.2 | async-start | bytes 2883584 | tf_op jit(solution)/shard_map/psum | solution.py:54
  12.5 90.8 %copy-start = (bf16[512,1408]{1,0:T(8,128)(2,1)S(1)}, bf16[512,1408]{1,0:T(8,128)(2,1)}, u32[]{:S(2)}) copy-start(bf16[512,1408]{1,0:T(8,128)(2,1)} %param.11) | copy-start | bytes 4325380
  12.5 90.8 %copy-start.8 = (f32[1408]{0:T(1024)S(1)}, f32[1408]{0:T(1024)}, u32[]{:S(2)}) copy-start(f32[1408]{0:T(1024)} %param.12) | copy-start | bytes 16900
  103.3 9.7 %copy-start.5 = (bf16[352,44]{0,1:T(8,128)(2,1)S(1)}, bf16[352,44]{0,1:T(8,128)(2,1)}, u32[]{:S(2)}) copy-start(bf16[352,44]{0,1:T(8,128)(2,1)} %param.14) | copy-start | bytes 92932
  107.2 1.0 copy-start.4
  108.4 112.3 %collective-permute-start = (bf16[256,2,352]{2,0,1:T(8,128)(2,1)S(1)}, bf16[256,2,352]{2,0,1:T(8,128)(2,1)S(1)}, u32[]{:S(2)}, u32[]{:S(2)}) collective-permute-start(bf16[256,2,352]{2,0,1:T(8,128)(2,1)S(1)} %copy.35), channel_id=1, source_target_pairs={{0,4},{4,8},{8,12},{12,16},{16,20},{20,24},{24,28},{28,32},{32,36}... | collective-permute-start | bytes 1081352 | tf_op jit(solution)/shard_map/ppermute | solution.py:21
  111.7 109.1 %collective-permute-start.1 = (bf16[256,2,352]{2,0,1:T(8,128)(2,1)}, bf16[256,2,352]{2,0,1:T(8,128)(2,1)}, u32[]{:S(2)}, u32[]{:S(2)}) collective-permute-start(bf16[256,2,352]{2,0,1:T(8,128)(2,1)} %copy.37), channel_id=1, source_target_pairs={{4,0},{8,4},{12,8},{16,12},{20,16},{24,20},{28,24},{32,28},{36,32}... | collective-permute-start | bytes 1081352 | tf_op jit(solution)/shard_map/ppermute | solution.py:24
  247.4 6.2 copy-start.2
  265.1 5.2 copy-start.3
  272.4 132.2 %all-gather.11.cloned.1.call-start = ((), (), s32[]{:S(2)}) async-start(), calls=%async_computation.4 | async-start | bytes 4866048 | tf_op jit(solution)/shard_map/all_gather | solution.py:66
  273.1 215.8 %all-gather.13.cloned.1.call-start = ((), (), s32[]{:S(2)}) async-start(), calls=%async_computation.5 | async-start | bytes 4866048 | tf_op jit(solution)/shard_map/all_gather | solution.py:67
  273.7 291.9 %all-gather.15.cloned.1.call-start = ((), (), s32[]{:S(2)}) async-start(), calls=%async_computation.6 | async-start | bytes 3244032 | tf_op jit(solution)/shard_map/all_gather | solution.py:68
  274.3 337.2 %all-reduce.5.cloned.1.call-start = ((), (), s32[]{:S(2)}) async-start(), calls=%async_computation.3 | async-start | bytes 2883584 | tf_op jit(solution)/shard_map/psum | solution.py:54
  315.9 1.9 copy-start.1
  411.7 84.3 %copy-start.9 = (f32[1408]{0:T(1024)S(1)}, f32[1408]{0:T(1024)}, u32[]{:S(2)}) copy-start(f32[1408]{0:T(1024)} %param.15) | copy-start | bytes 16900
  496.0 15.1 %copy-start.7 = (s32[512]{0:T(512)S(1)}, s32[512]{0:T(512)}, u32[]{:S(2)}) copy-start(s32[512]{0:T(512)} %param.20) | copy-start | bytes 6148
  496.0 15.2 %copy-start.6 = (s32[128,1]{0,1:T(1,128)S(1)}, s32[128,1]{0,1:T(1,128)}, u32[]{:S(2)}) copy-start(s32[128,1]{0,1:T(1,128)} %param.21) | copy-start | bytes 1540
Sparse Core Ops, SparseCore 0:
  10.3 85.2 all-gather.8
  272.5 43.3 all-reduce.2
  318.9 85.6 all-gather.10
  407.4 81.4 all-gather.12
  491.7 73.8 all-gather.14
  568.0 43.4 all-reduce.4
where the time goes:
time: 649 us; the launch traced here: 648 us
  waiting for transfers between devices  384 us (59%)
  blocking collectives  125 us (19%)
  local copies, waits for them, and re-layouts  75.8 us (12%)
  matrix products  31.7 us (5%)
  between operations  13.7 us (2%)
  other arithmetic  13.3 us (2%)
    all_gather x1, blocking collectives, body(): lax.all_gather(w_out, 'tm', axis=1, tiled=True)  102 us
    all_gather x1, waiting for transfers between devices, body(): lax.all_gather(w_up, 'tm', axis=0, tiled=True)  86.1 us
    all_gather x1, waiting for transfers between devices, body(): lax.all_gather(w_qkv, 'tm', axis=0, tiled=True)  83.1 us
    psum x2, waiting for transfers between devices, tensor_total(): return lax.psum(term.astype(jnp.bfloat16), 'tensor').astype(jnp.float32)  82 us
    all_gather x1, waiting for transfers between devices, body(): lax.all_gather(w_down, 'tm', axis=1, tiled=True)  77.3 us
    all_gather x1, waiting for transfers between devices, body(): lax.all_gather(w_proj, 'tm', axis=0, tiled=True)  54 us
    unnamed x31, local copies, waits for them, and re-layouts  38.5 us
    all_to_all x1, blocking collectives, body(): lax.all_to_all(outbox, 'tm', split_axis=0, concat_axis=0, tiled=True)  23.1 us
  transfers between devices with their start and end apart: 8, of which 6 were waited for; matrix products, arithmetic and copies ran while one was open for 7% of the time, Pallas kernels for 0%

commit v1 on v0

--- a/solution.py
+++ b/solution.py
@@ -51,7 +51,7 @@
 
 
 def tensor_total(term):
-    return lax.psum(term.astype(jnp.bfloat16), "tensor").astype(jnp.float32)
+    return jnp.sum(lax.all_gather(term.astype(jnp.bfloat16), "tensor"), axis=0).astype(jnp.float32)
 
 
 def body(

time: 649 us -> 517 us (0.80)
  waiting for transfers between devices: 384 us -> 240 us
  other arithmetic: 13.3 us -> 23 us
    all_gather x0 -> x2, waiting for transfers between devices: none -> 95 us  [tensor_total(): lax.all_gather(term.astype(jnp.bfloat16), 'tensor')]
    all_gather x1, waiting for transfers between devices: 86.1 us -> 0.02 us  [body(): lax.all_gather(w_up, 'tm', axis=0, tiled=True)]
    psum x2 -> x0, waiting for transfers between devices: 82 us -> none  [tensor_total(): return lax.psum(term.astype(jnp.bfloat16), 'tensor').astype(jnp.float32)]
    all_gather x1, waiting for transfers between devices: 77.3 us -> 0.01 us  [body(): lax.all_gather(w_down, 'tm', axis=1, tiled=True)]
    reduce_sum x0 -> x2, other arithmetic: none -> 9.39 us  [tensor_total(): jnp.sum(lax.all_gather(term.astype(jnp.bfloat16), 'tensor'), axis=0)]
  transfers between devices with their start and end apart: 8 -> 8, of which waited for: 6 -> 4; matrix products, arithmetic and copies ran while one was open for 7% -> 22% of each run, Pallas kernels for 0% -> 0%
where the time goes in v1:
time: 517 us; the launch traced here: 515 us
  waiting for transfers between devices  240 us (46%)
  blocking collectives  129 us (25%)
  local copies, waits for them, and re-layouts  76.8 us (15%)
  matrix products  28.7 us (6%)
  other arithmetic  23 us (4%)
  between operations  13.7 us (3%)
    all_gather x1, blocking collectives, body(): lax.all_gather(w_out, 'tm', axis=1, tiled=True)  105 us
    all_gather x2, waiting for transfers between devices, tensor_total(): lax.all_gather(term.astype(jnp.bfloat16), 'tensor')  95 us
    all_gather x1, waiting for transfers between devices, body(): lax.all_gather(w_qkv, 'tm', axis=0, tiled=True)  82.8 us
    all_gather x1, waiting for transfers between devices, body(): lax.all_gather(w_proj, 'tm', axis=0, tiled=True)  60.4 us
    unnamed x31, local copies, waits for them, and re-layouts  38.9 us
    all_to_all x1, blocking collectives, body(): lax.all_to_all(outbox, 'tm', split_axis=0, concat_axis=0, tiled=True)  23.9 us
    dot_general x1, matrix products, body(): jnp.dot(activation, full_down, preferred_element_type=jnp.float32)  15.2 us
    gather x2, local copies, waits for them, and re-layouts, attend_group(): kv_blocks[id_group].reshape(group_size, WIN * BLK, 2, heads_here, head_dim)  15 us
  transfers between devices with their start and end apart: 8, of which 4 were waited for; matrix products, arithmetic and copies ran while one was open for 22% of the time, Pallas kernels for 0%

profile of v1, /device:TPU:0, one launch (start us, length us, event | category | flops | bytes accessed | tf_op | source)
XLA Modules:
  0.0 514.9 jit_solution(17916478248998559553)
XLA Ops:
  6.5 1.7 copy.23
  10.6 1.6 convert_reduce_fusion
  12.8 82.8 %all-gather.13.cloned.1.call-done = bf16[1408,3,352]{2,1,0:T(4,128)(2,1)} async-done(((bf16[44,3,352]{2,1,0:T(4,128)(2,1)}), bf16[1408,3,352]{2,1,0:T(4,128)(2,1)}) %all-gather.13.cloned.1.call-update) | async-done | bytes 2973712 | tf_op jit(solution)/shard_map/all_gather | solution.py:64
  95.6 7.7 %copy.24 = bf16[1408,3,352]{0,2,1:T(8,128)(2,1)} copy(bf16[1408,3,352]{2,1,0:T(4,128)(2,1)} %all-gather.13.cloned.1.call-done) | data formatting | bytes 5947392 | tf_op jit(solution)/shard_map/all_gather | solution.py:64
  103.3 3.9 convolution_convert_fusion.2
  108.4 2.3 collective-permute-start
  111.7 1.3 collective-permute-start.1
  113.0 104.7 %all-gather.2 = bf16[32,44,352]{2,1,0:T(8,128)(2,1)S(1)} all-gather(bf16[1,44,352]{2,1,0:T(8,128)(2,1)S(1)} %bitcast.57), channel_id=1, replica_groups=mesh['tm'=32,'tensor'=4] {'tm'}, dimensions={0}, use_global_device_ids=true | all-gather | bytes 1022208 | tf_op jit(solution)/shard_map/all_gather | solution.py:65
  223.5 1.4 pad_maximum_fusion
  224.9 2.3 reshape.72
  227.2 2.2 copy.28
  229.3 5.6 %gather_fusion = bf16[64,64,2,4,88]{4,1,3,2,0:T(8,128)(2,1)} fusion(bf16[16,64,2,4,88]{4,1,3,2,0:T(8,128)(2,1)S(1)} %copy.28, s32[1024]{0:T(1024)S(1)} %pad_clamp_fusion), kind=kCustom, calls=%fused_computation | custom fusion | bytes 11534592 | tf_op jit(solution)/shard_map/while/body/eval_jaxpr/gather | solution.py:89
  234.9 9.4 %copy.29 = bf16[64,64,2,4,88]{4,1,0,3,2:T(8,128)(2,1)} copy(bf16[64,64,2,4,88]{4,1,3,2,0:T(8,128)(2,1)} %gather_fusion) | data formatting | bytes 11534336 | tf_op jit(solution)/shard_map/while/body/eval_jaxpr/gather | solution.py:89
  244.3 6.4 %fusion.110 = (bf16[8,512,1,4,88]{4,1,0,3,2:T(8,128)(2,1)}, bf16[8,512,1,4,88]{4,1,0,3,2:T(8,128)(2,1)}) fusion(bf16[8,512,2,4,88]{4,1,0,3,2:T(8,128)(2,1)} %bitcast.44), kind=kLoop, calls=%fused_computation.136 | loop fusion | bytes 11534336 | tf_op jit(solution)/shard_map/while/body/eval_jaxpr/slice | solution.py:100
  250.7 6.1 %copy.40 = bf16[8,512,1,4,88]{1,4,3,0,2:T(8,128)(2,1)} copy(bf16[8,512,1,4,88]{4,1,0,3,2:T(8,128)(2,1)} %get-tuple-element.14) | data formatting | bytes 5767168
  256.8 6.2 %copy.38 = bf16[8,512,1,4,88]{1,4,3,0,2:T(8,128)(2,1)} copy(bf16[8,512,1,4,88]{4,1,0,3,2:T(8,128)(2,1)} %get-tuple-element.13) | data formatting | bytes 5767168
  263.0 2.6 fusion.19
  265.6 6.0 %fusion.112 = (f32[8,4,64]{2,1,0:T(4,128)S(1)}, f32[8,4,64,512]{3,2,1,0:T(8,128)S(1)}) fusion(f32[8,4,64,512]{3,2,1,0:T(8,128)S(1)} %fusion.19), kind=kOutput, calls=%fused_computation.138 | output fusion | flops 4194815 | bytes 8396800 | tf_op jit(solution)/shard_map/while/body/eval_jaxpr/sub | solution.py:97
  271.6 1.3 fusion.72
  273.6 2.0 convolution_convert_fusion.1
  276.3 7.0 %reshape.94 = bf16[1408,1536]{1,0:T(8,128)(2,1)} reshape(bf16[32,44,1536]{2,1,0:T(8,128)(2,1)} %all-gather.19.cloned.1.call-done) | data formatting | bytes 8650752
  283.4 7.4 %reshape.96 = bf16[1408,1536]{1,0:T(8,128)(2,1)} reshape(bf16[32,44,1536]{2,1,0:T(8,128)(2,1)} %all-gather.21.cloned.1.call-done) | data formatting | bytes 8650752
  290.8 43.3 %all-gather.15.cloned.1.call-done = bf16[2048,1408]{1,0:T(8,128)(2,1)} async-done(((bf16[512,1408]{1,0:T(8,128)(2,1)}), bf16[2048,1408]{1,0:T(8,128)(2,1)}) %all-gather.15.cloned.1.call-update) | async-done | bytes 5767184 | tf_op jit(solution)/shard_map/all_gather | solution.py:54
  334.1 4.4 reduce_sum.83
  339.6 15.2 %convolution_convert_fusion = bf16[512,1408]{1,0:T(8,128)(2,1)} fusion(bf16[1408,1536]{1,0:T(8,128)(2,1)} %reshape.96, bf16[1408,1536]{1,0:T(8,128)(2,1)} %reshape.94, bf16[512,1408]{1,0:T(8,128)(2,1)S(1)} %reduce_sum.83, bf16[512,1408]{1,0:T(8,128)(2,1)S(1)} %copy-done, f32[1408]{0:T(1024)S(1)} %copy-done.9, f32[512]{0:T(512)S(1)} %add_rsqrt_fusion, ...), kind=kOutput, calls=%fused_computation.30 | convolution fusion | flops 4486070272 | bytes 12985856 | tf_op jit(solution)/shard_map/dot_general | solution.py:113
  355.4 60.4 %all-gather.23.cloned.1.call-done = bf16[32,44,1024]{2,1,0:T(8,128)(2,1)} async-done(((bf16[1,44,1024]{2,1,0:T(8,128)(2,1)}), bf16[32,44,1024]{2,1,0:T(8,128)(2,1)}) %all-gather.23.cloned.1.call-update) | async-done | bytes 2883600 | tf_op jit(solution)/shard_map/all_gather | solution.py:68
  415.8 5.3 %reshape.98 = bf16[1408,1024]{1,0:T(8,128)(2,1)} reshape(bf16[32,44,1024]{2,1,0:T(8,128)(2,1)} %all-gather.23.cloned.1.call-done) | data formatting | bytes 5767168
  421.0 51.7 %all-gather.17.cloned.1.call-done = bf16[2048,1408]{1,0:T(8,128)(2,1)} async-done(((bf16[512,1408]{1,0:T(8,128)(2,1)}), bf16[2048,1408]{1,0:T(8,128)(2,1)}) %all-gather.17.cloned.1.call-update) | async-done | bytes 5767184 | tf_op jit(solution)/shard_map/all_gather | solution.py:54
  472.8 5.0 reduce_sum.86
  477.8 1.8 convert_add_fusion.1
  480.7 2.6 fusion.71
  483.3 23.9 %all_to_all.5 = bf16[32,8,1024]{2,1,0:T(8,128)(2,1)S(1)} all-to-all(bf16[32,8,1024]{2,1,0:T(8,128)(2,1)S(1)} %fusion.71), channel_id=1, replica_groups=mesh['tm'=32,'tensor'=4] {'tm'}, dimensions={0} | all-to-all | bytes 1048576 | tf_op jit(solution)/shard_map/all_to_all | solution.py:131
  (63 shorter events, 15.7 us)
Async XLA Ops:
  6.5 5.7 %copy-start = (bf16[512,1408]{1,0:T(8,128)(2,1)S(1)}, bf16[512,1408]{1,0:T(8,128)(2,1)}, u32[]{:S(2)}) copy-start(bf16[512,1408]{1,0:T(8,128)(2,1)} %param.11) | copy-start | bytes 4325380
  6.5 89.1 %all-gather.13.cloned.1.call-start = ((), (), s32[]{:S(2)}) async-start(), calls=%async_computation.1 | async-start | bytes 4460544 | tf_op jit(solution)/shard_map/all_gather | solution.py:64
  8.3 268.1 %all-gather.19.cloned.1.call-start = ((), (), s32[]{:S(2)}) async-start(), calls=%async_computation.4 | async-start | bytes 4866048 | tf_op jit(solution)/shard_map/all_gather | solution.py:66
  9.0 274.4 %all-gather.21.cloned.1.call-start = ((), (), s32[]{:S(2)}) async-start(), calls=%async_computation.5 | async-start | bytes 4866048 | tf_op jit(solution)/shard_map/all_gather | solution.py:67
  9.8 324.3 %all-gather.15.cloned.1.call-start = ((), (), s32[]{:S(2)}) async-start(), calls=%async_computation.2 | async-start | bytes 7208960 | tf_op jit(solution)/shard_map/all_gather | solution.py:54
  12.8 90.5 %copy-start.8 = (f32[1408]{0:T(1024)S(1)}, f32[1408]{0:T(1024)}, u32[]{:S(2)}) copy-start(f32[1408]{0:T(1024)} %param.12) | copy-start | bytes 16900
  103.3 9.7 %copy-start.5 = (bf16[352,44]{0,1:T(8,128)(2,1)S(1)}, bf16[352,44]{0,1:T(8,128)(2,1)}, u32[]{:S(2)}) copy-start(bf16[352,44]{0,1:T(8,128)(2,1)} %param.14) | copy-start | bytes 92932
  107.2 1.0 copy-start.3
  108.4 115.0 %collective-permute-start = (bf16[256,2,352]{2,0,1:T(8,128)(2,1)S(1)}, bf16[256,2,352]{2,0,1:T(8,128)(2,1)S(1)}, u32[]{:S(2)}, u32[]{:S(2)}) collective-permute-start(bf16[256,2,352]{2,0,1:T(8,128)(2,1)S(1)} %copy.35), channel_id=1, source_target_pairs={{0,4},{4,8},{8,12},{12,16},{16,20},{20,24},{24,28},{28,32},{32,36}... | collective-permute-start | bytes 1081352 | tf_op jit(solution)/shard_map/ppermute | solution.py:21
  111.7 111.8 %collective-permute-start.1 = (bf16[256,2,352]{2,0,1:T(8,128)(2,1)}, bf16[256,2,352]{2,0,1:T(8,128)(2,1)}, u32[]{:S(2)}, u32[]{:S(2)}) collective-permute-start(bf16[256,2,352]{2,0,1:T(8,128)(2,1)} %copy.37), channel_id=1, source_target_pairs={{4,0},{8,4},{12,8},{16,12},{20,16},{24,20},{28,24},{32,28},{36,32}... | collective-permute-start | bytes 1081352 | tf_op jit(solution)/shard_map/ppermute | solution.py:24
  256.8 6.2 %copy-start.1 = (bf16[8,64,4,88]{1,0,3,2:T(8,128)(2,1)S(1)}, bf16[8,64,4,88]{1,0,3,2:T(8,128)(2,1)}, u32[]{:S(2)}) copy-start(bf16[8,64,4,88]{1,0,3,2:T(8,128)(2,1)} %reshape.99) | copy-start | bytes 1081348
  265.6 6.0 %copy-start.4 = (bf16[8,512,1,4,88]{1,4,3,0,2:T(8,128)(2,1)S(1)}, bf16[8,512,1,4,88]{1,4,3,0,2:T(8,128)(2,1)}, u32[]{:S(2)}) copy-start(bf16[8,512,1,4,88]{1,4,3,0,2:T(8,128)(2,1)} %copy.38) | copy-start | bytes 8650756
  271.5 2.1 copy-start.2
  275.7 140.1 %all-gather.23.cloned.1.call-start = ((), (), s32[]{:S(2)}) async-start(), calls=%async_computation.6 | async-start | bytes 3244032 | tf_op jit(solution)/shard_map/all_gather | solution.py:68
  276.3 196.5 %all-gather.17.cloned.1.call-start = ((), (), s32[]{:S(2)}) async-start(), calls=%async_computation.3 | async-start | bytes 7208960 | tf_op jit(solution)/shard_map/all_gather | solution.py:54
  338.4 1.1 copy-start.9
  339.6 15.3 %copy-start.7 = (s32[512]{0:T(512)S(1)}, s32[512]{0:T(512)}, u32[]{:S(2)}) copy-start(s32[512]{0:T(512)} %param.20) | copy-start | bytes 6148
  339.6 15.3 %copy-start.6 = (s32[128,1]{0,1:T(1,128)S(1)}, s32[128,1]{0,1:T(1,128)}, u32[]{:S(2)}) copy-start(s32[128,1]{0,1:T(1,128)} %param.21) | copy-start | bytes 1540
Sparse Core Ops, SparseCore 0:
  10.3 85.2 all-gather.12
  98.5 94.0 all-gather.18
  195.6 81.3 all-gather.20
  278.5 55.5 all-gather.14
  336.9 78.8 all-gather.22
  417.3 55.4 all-gather.16
